TPU v7x, 32 devices: a whole 2x2x4 slice. The times are simulated.
32 devices in a mesh: grp: 2 (over y), col: 4 (over z), seq: 4 (over x, core).
Axes of the slice: x: 2, y: 2, z: 4, core: 2. Of those that a mesh axis runs over, the one named last changes fastest.
Arguments:
- row_query: bfloat16 [256, 16, 768], P(('grp', 'seq'), 'col'), parts along dimension 0, may hold values from -6 to 6
- row_key: bfloat16 [256, 16, 768], P(('grp', 'seq'), 'col'), parts along dimension 0, may hold values from -6 to 6
- row_value: bfloat16 [256, 16, 768], P(('grp', 'seq'), 'col'), parts along dimension 0, may hold values from -6 to 6
- row_grad: bfloat16 [256, 16, 768], P(('grp', 'seq'), 'col'), parts along dimension 0, may hold values from -48 to 48
- col_query: bfloat16 [256, 16, 768], P(('grp', 'seq'), 'col'), parts along dimension 0, may hold values from -11 to 11
- col_key: bfloat16 [256, 16, 768], P(('grp', 'seq'), 'col'), parts along dimension 0, may hold values from -11 to 11
- col_value: bfloat16 [256, 16, 768], P(('grp', 'seq'), 'col'), parts along dimension 0, may hold values from -6 to 6
- col_grad: bfloat16 [256, 16, 768], P(('grp', 'seq'), 'col'), parts along dimension 0, may hold values from -48 to 48
Outputs:
- row_dquery: bfloat16 [256, 16, 768], P(('grp', 'seq'), 'col'), parts along dimension 0
- row_dkey: bfloat16 [256, 16, 768], P(('grp', 'seq'), 'col'), parts along dimension 0
- row_dvalue: bfloat16 [256, 16, 768], P(('grp', 'seq'), 'col'), parts along dimension 0
- col_dquery: bfloat16 [256, 16, 768], P(('grp', 'seq'), 'col'), parts along dimension 0
- col_dkey: bfloat16 [256, 16, 768], P(('grp', 'seq'), 'col'), parts along dimension 0
- col_dvalue: bfloat16 [256, 16, 768], P(('grp', 'seq'), 'col'), parts along dimension 0
There are 2 independent parts, one for each index of `grp`. A program takes and returns all parts, laid end to end along the dimension named above; each array names one. Nothing has to cross between parts.
All inputs are finite; a program needn't handle non-finite values.
Results may differ from a plain program's by a relative error of at most 0.009.
Values may be sent and summed in bfloat16 or wider, within the bound.
No kernel may reach another device: no remote copies, remote signals or barrier semaphores. Data moves between devices by JAX's collectives and lax.ppermute only.
A program may use at most 64 MiB of HBM per device.

v0:
```python
import jax
import jax.numpy as jnp
from jax import lax
from jax.sharding import PartitionSpec as P

HEADS = 12
HEAD = 64


def tied_terms(scores, prob_grad, row_scale):
    row_probs = jax.nn.softmax(scores, axis=-1)
    row_delta = jnp.sum(row_probs * prob_grad, axis=-1, keepdims=True)
    score_gradient_part = row_probs * (prob_grad - row_delta) * row_scale
    return (row_probs.astype(jnp.bfloat16), score_gradient_part.astype(jnp.bfloat16))


def split_heads(block):
    return block.reshape(block.shape[0], block.shape[1] // HEAD, HEAD)


def column_core(query_row_block, key_row_block, value_row_block, gradient_row_block, col_scale):
    scores = (
        jnp.einsum(
            "qzd,izd->zqi", query_row_block, key_row_block, preferred_element_type=jnp.float32
        )
        * col_scale
    )
    prob_grad = jnp.einsum(
        "qzd,izd->zqi", gradient_row_block, value_row_block, preferred_element_type=jnp.float32
    )
    col_probs = jax.nn.softmax(scores, axis=-1)
    col_delta = jnp.sum(col_probs * prob_grad, axis=-1, keepdims=True)
    score_gradient_part = (col_probs * (prob_grad - col_delta) * col_scale).astype(jnp.bfloat16)
    attention_weight_rows = col_probs.astype(jnp.bfloat16)
    query_grad = jnp.einsum(
        "qvc,cqb->vqb", score_gradient_part, key_row_block, preferred_element_type=jnp.float32
    )
    key_gradient_part = jnp.einsum(
        "wzc,zwi->cwi", score_gradient_part, query_row_block, preferred_element_type=jnp.float32
    )
    value_gradient_part = jnp.einsum(
        "wzc,zwi->cwi",
        attention_weight_rows,
        gradient_row_block,
        preferred_element_type=jnp.float32,
    )
    return (
        query_grad.astype(jnp.bfloat16),
        key_gradient_part.astype(jnp.bfloat16),
        value_gradient_part.astype(jnp.bfloat16),
    )


def local(row_query, row_key, row_value, row_grad, col_query, col_key, col_value, col_grad):
    seq_dev, col_dev, width = row_query.shape
    seqs = seq_dev * lax.axis_size("seq")
    cols = col_dev * lax.axis_size("col")
    row_scale = HEAD ** (-0.5) * seqs ** (-0.5)
    col_scale = HEAD ** (-0.5)
    moved = (
        lax.all_to_all(row_query, "col", split_axis=0, concat_axis=1, tiled=True),
        lax.all_to_all(row_key, "col", split_axis=0, concat_axis=1, tiled=True),
        lax.all_to_all(row_value, "col", split_axis=0, concat_axis=1, tiled=True),
        lax.all_to_all(row_grad, "col", split_axis=0, concat_axis=1, tiled=True),
    )
    own_rows = moved[0].shape[0]
    shape_four = (own_rows, cols, HEADS, HEAD)
    query_row_block = moved[0].reshape(shape_four)
    key_row_block = moved[1].reshape(shape_four)
    value_row_block = moved[2].reshape(shape_four)
    gradient_row_block = moved[3].reshape(shape_four)
    score_part = (
        jnp.einsum(
            "sihe,sjhe->hij", query_row_block, key_row_block, preferred_element_type=jnp.float32
        )
        * row_scale
    )
    prob_part = jnp.einsum(
        "sihe,sjhe->hij", gradient_row_block, value_row_block, preferred_element_type=jnp.float32
    )
    scores, prob_grad = lax.psum((score_part, prob_part), ("col", "seq"))
    attention_weight_rows, score_gradient_part = tied_terms(scores, prob_grad, row_scale)
    query_grad = jnp.einsum(
        "hij,sjhe->sihe", score_gradient_part, key_row_block, preferred_element_type=jnp.float32
    )
    key_gradient_part = jnp.einsum(
        "hij,sihe->sjhe", score_gradient_part, query_row_block, preferred_element_type=jnp.float32
    )
    value_gradient_part = jnp.einsum(
        "hij,sihe->sjhe",
        attention_weight_rows,
        gradient_row_block,
        preferred_element_type=jnp.float32,
    )
    row_back = (
        lax.all_to_all(
            query_grad.astype(jnp.bfloat16).reshape(own_rows, cols, width),
            "col",
            split_axis=1,
            concat_axis=0,
            tiled=True,
        ),
        lax.all_to_all(
            key_gradient_part.astype(jnp.bfloat16).reshape(own_rows, cols, width),
            "col",
            split_axis=1,
            concat_axis=0,
            tiled=True,
        ),
        lax.all_to_all(
            value_gradient_part.astype(jnp.bfloat16).reshape(own_rows, cols, width),
            "col",
            split_axis=1,
            concat_axis=0,
            tiled=True,
        ),
    )
    flat_width = col_dev * width
    col_moved = (
        lax.all_to_all(
            col_query.reshape(seq_dev, flat_width), "seq", split_axis=1, concat_axis=0, tiled=True
        ),
        lax.all_to_all(
            col_key.reshape(seq_dev, flat_width), "seq", split_axis=1, concat_axis=0, tiled=True
        ),
        lax.all_to_all(
            col_value.reshape(seq_dev, flat_width), "seq", split_axis=1, concat_axis=0, tiled=True
        ),
        lax.all_to_all(
            col_grad.reshape(seq_dev, flat_width), "seq", split_axis=1, concat_axis=0, tiled=True
        ),
    )
    col_grads = column_core(
        split_heads(col_moved[0]),
        split_heads(col_moved[1]),
        split_heads(col_moved[2]),
        split_heads(col_moved[3]),
        col_scale,
    )
    share_width = col_moved[0].shape[1]
    col_back = (
        lax.all_to_all(
            col_grads[0].reshape(seqs, share_width), "seq", split_axis=0, concat_axis=1, tiled=True
        ),
        lax.all_to_all(
            col_grads[1].reshape(seqs, share_width), "seq", split_axis=0, concat_axis=1, tiled=True
        ),
        lax.all_to_all(
            col_grads[2].reshape(seqs, share_width), "seq", split_axis=0, concat_axis=1, tiled=True
        ),
    )
    return (
        row_back[0],
        row_back[1],
        row_back[2],
        col_back[0].reshape(seq_dev, col_dev, width),
        col_back[1].reshape(seq_dev, col_dev, width),
        col_back[2].reshape(seq_dev, col_dev, width),
    )


def solution(mesh):
    in_specs = (
        P(("grp", "seq"), "col", None),
        P(("grp", "seq"), "col", None),
        P(("grp", "seq"), "col", None),
        P(("grp", "seq"), "col", None),
        P(("grp", "seq"), "col", None),
        P(("grp", "seq"), "col", None),
        P(("grp", "seq"), "col", None),
        P(("grp", "seq"), "col", None),
    )
    out_specs = (
        P(("grp", "seq"), "col", None),
        P(("grp", "seq"), "col", None),
        P(("grp", "seq"), "col", None),
        P(("grp", "seq"), "col", None),
        P(("grp", "seq"), "col", None),
        P(("grp", "seq"), "col", None),
    )
    return jax.shard_map(local, mesh=mesh, in_specs=in_specs, out_specs=out_specs, check_vma=False)
```

profile of v0, /device:TPU:0, one launch (start us, length us, event | category | flops | bytes accessed | tf_op | source)
XLA Modules:
  0.0 195.9 jit_solution(17410516336404553708)
XLA Ops:
  0.6 1.6 copy.133
  2.3 4.3 %all-to-all-start.8 = ((bf16[32,4,768]{2,0,1:T(8,128)(2,1)}), bf16[32,4,768]{2,0,1:T(8,128)(2,1)S(1)}, u32[]{:S(2)}, u32[]{:S(2)}) async-start(bf16[32,4,768]{2,0,1:T(8,128)(2,1)} %copy.133), calls=%async_computation.8 | async-start | bytes 393216 | tf_op jit(solution)/shard_map/all_to_all | solution.py:123
  7.3 4.6 %all-to-all-done.8 = bf16[32,4,768]{2,0,1:T(8,128)(2,1)S(1)} async-done(((bf16[32,4,768]{2,0,1:T(8,128)(2,1)}), bf16[32,4,768]{2,0,1:T(8,128)(2,1)S(1)}, u32[]{:S(2)}, u32[]{:S(2)}) %all-to-all-start.8) | async-done | bytes 196640 | tf_op jit(solution)/shard_map/all_to_all | solution.py:123
  11.9 3.4 %all-to-all-start.9 = ((bf16[32,4,768]{2,0,1:T(8,128)(2,1)}), bf16[32,4,768]{2,0,1:T(8,128)(2,1)S(1)}, u32[]{:S(2)}, u32[]{:S(2)}) async-start(bf16[32,4,768]{2,0,1:T(8,128)(2,1)} %copy.136), calls=%async_computation.9 | async-start | bytes 393216 | tf_op jit(solution)/shard_map/all_to_all | solution.py:129
  16.0 4.6 %all-to-all-done.9 = bf16[32,4,768]{2,0,1:T(8,128)(2,1)S(1)} async-done(((bf16[32,4,768]{2,0,1:T(8,128)(2,1)}), bf16[32,4,768]{2,0,1:T(8,128)(2,1)S(1)}, u32[]{:S(2)}, u32[]{:S(2)}) %all-to-all-start.9) | async-done | bytes 196640 | tf_op jit(solution)/shard_map/all_to_all | solution.py:129
  20.6 3.4 %all-to-all-start.10 = ((bf16[32,4,768]{2,0,1:T(8,128)(2,1)}), bf16[32,4,768]{2,0,1:T(8,128)(2,1)S(1)}, u32[]{:S(2)}, u32[]{:S(2)}) async-start(bf16[32,4,768]{2,0,1:T(8,128)(2,1)} %copy.137), calls=%async_computation.10 | async-start | bytes 393216 | tf_op jit(solution)/shard_map/all_to_all | solution.py:126
  24.0 5.2 %all-to-all-done.10 = bf16[32,4,768]{2,0,1:T(8,128)(2,1)S(1)} async-done(((bf16[32,4,768]{2,0,1:T(8,128)(2,1)}), bf16[32,4,768]{2,0,1:T(8,128)(2,1)S(1)}, u32[]{:S(2)}, u32[]{:S(2)}) %all-to-all-start.10) | async-done | bytes 196640 | tf_op jit(solution)/shard_map/all_to_all | solution.py:126
  29.3 7.7 %all_to_all.214 = bf16[32,4,768]{2,0,1:T(8,128)(2,1)S(1)} all-to-all(bf16[32,4,768]{2,0,1:T(8,128)(2,1)S(1)} %copy.132), channel_id=1, replica_groups=mesh['grp'=2,'col'=4,'seq'=4] {'seq'}, dimensions={1} | all-to-all | bytes 393216 | tf_op jit(solution)/shard_map/all_to_all | solution.py:120
  37.0 12.7 %all_to_all.215 = bf16[32,4,768]{2,1,0:T(4,128)(2,1)S(1)} all-to-all(bf16[32,4,768]{2,1,0:T(4,128)(2,1)S(1)} %copy-done.3), channel_id=1, replica_groups=mesh['grp'=2,'col'=4,'seq'=4] {'col'}, dimensions={0} | all-to-all | bytes 393216 | tf_op jit(solution)/shard_map/all_to_all | solution.py:63
  49.7 3.4 %all-to-all-start.2 = ((bf16[32,4,768]{2,1,0:T(4,128)(2,1)}), bf16[32,4,768]{2,1,0:T(4,128)(2,1)S(1)}, u32[]{:S(2)}, u32[]{:S(2)}) async-start(bf16[32,4,768]{2,1,0:T(4,128)(2,1)} %param.11), calls=%async_computation.2 | async-start | bytes 393216 | tf_op jit(solution)/shard_map/all_to_all | solution.py:64
  55.8 3.5 %all-to-all-done.2 = bf16[32,4,768]{2,1,0:T(4,128)(2,1)S(1)} async-done(((bf16[32,4,768]{2,1,0:T(4,128)(2,1)}), bf16[32,4,768]{2,1,0:T(4,128)(2,1)S(1)}, u32[]{:S(2)}, u32[]{:S(2)}) %all-to-all-start.2) | async-done | bytes 196640 | tf_op jit(solution)/shard_map/all_to_all | solution.py:64
  59.4 3.4 %all-to-all-start.1 = ((bf16[32,4,768]{2,1,0:T(4,128)(2,1)}), bf16[32,4,768]{2,1,0:T(4,128)(2,1)S(1)}, u32[]{:S(2)}, u32[]{:S(2)}) async-start(bf16[32,4,768]{2,1,0:T(4,128)(2,1)} %param.9), calls=%async_computation.1 | async-start | bytes 393216 | tf_op jit(solution)/shard_map/all_to_all | solution.py:62
  63.5 5.4 %all-to-all-done.1 = bf16[32,4,768]{2,1,0:T(4,128)(2,1)S(1)} async-done(((bf16[32,4,768]{2,1,0:T(4,128)(2,1)}), bf16[32,4,768]{2,1,0:T(4,128)(2,1)S(1)}, u32[]{:S(2)}, u32[]{:S(2)}) %all-to-all-start.1) | async-done | bytes 196640 | tf_op jit(solution)/shard_map/all_to_all | solution.py:62
  68.9 3.4 %all-to-all-start = ((bf16[32,4,768]{2,1,0:T(4,128)(2,1)}), bf16[32,4,768]{2,1,0:T(4,128)(2,1)S(1)}, u32[]{:S(2)}, u32[]{:S(2)}) async-start(bf16[32,4,768]{2,1,0:T(4,128)(2,1)} %param.8), calls=%async_computation | async-start | bytes 393216 | tf_op jit(solution)/shard_map/all_to_all | solution.py:61
  73.1 1.0 all_to_all.191
  74.6 1.0 all_to_all.194
  76.6 1.0 all_to_all.197
  78.7 3.4 %all-to-all-start.11 = ((bf16[4,32,768]{2,1,0:T(8,128)(2,1)}), bf16[4,32,768]{2,1,0:T(8,128)(2,1)S(1)}, u32[]{:S(2)}, u32[]{:S(2)}) async-start(bf16[4,32,768]{2,1,0:T(8,128)(2,1)} %all_to_all.191), calls=%async_computation.11 | async-start | bytes 393216 | tf_op jit(solution)/shard_map/all_to_all | solution.py:142
  83.5 64.1 %all-reduce = (f32[12,16,16]{2,1,0:T(8,128)S(1)}, f32[12,16,16]{2,1,0:T(8,128)S(1)}) all-reduce(f32[12,16,16]{2,1,0:T(8,128)S(1)} %convolution_bitcast_fusion, f32[12,16,16]{2,1,0:T(8,128)S(1)} %fusion.21), channel_id=1, replica_groups=mesh['grp'=2,'col'=4,'seq'=4] {'col','seq'}, use_global_device_ids=true, to_apply=%region_3.0 | all-reduce | flops 6144 | bytes 49152 | tf_op jit(solution)/shard_map/psum | solution.py:81
  147.6 3.4 %all-to-all-start.12 = ((bf16[4,32,768]{2,1,0:T(8,128)(2,1)}), bf16[4,32,768]{2,1,0:T(8,128)(2,1)S(1)}, u32[]{:S(2)}, u32[]{:S(2)}) async-start(bf16[4,32,768]{2,1,0:T(8,128)(2,1)} %all_to_all.194), calls=%async_computation.12 | async-start | bytes 393216 | tf_op jit(solution)/shard_map/all_to_all | solution.py:145
  151.0 1.9 fusion.58
  152.9 3.4 %all-to-all-done.12 = bf16[4,32,768]{2,1,0:T(8,128)(2,1)S(1)} async-done(((bf16[4,32,768]{2,1,0:T(8,128)(2,1)}), bf16[4,32,768]{2,1,0:T(8,128)(2,1)S(1)}, u32[]{:S(2)}, u32[]{:S(2)}) %all-to-all-start.12) | async-done | bytes 196640 | tf_op jit(solution)/shard_map/all_to_all | solution.py:145
  156.3 3.4 %all-to-all-start.13 = ((bf16[4,32,768]{2,1,0:T(8,128)(2,1)}), bf16[4,32,768]{2,1,0:T(8,128)(2,1)S(1)}, u32[]{:S(2)}, u32[]{:S(2)}) async-start(bf16[4,32,768]{2,1,0:T(8,128)(2,1)} %all_to_all.197), calls=%async_computation.13 | async-start | bytes 393216 | tf_op jit(solution)/shard_map/all_to_all | solution.py:148
  160.7 1.0 reshape.116
  161.7 3.3 %all-to-all-done.13 = bf16[4,32,768]{2,1,0:T(8,128)(2,1)S(1)} async-done(((bf16[4,32,768]{2,1,0:T(8,128)(2,1)}), bf16[4,32,768]{2,1,0:T(8,128)(2,1)S(1)}, u32[]{:S(2)}, u32[]{:S(2)}) %all-to-all-start.13) | async-done | bytes 196640 | tf_op jit(solution)/shard_map/all_to_all | solution.py:148
  165.0 3.5 %all-to-all-start.4 = ((bf16[8,16,768]{2,0,1:T(8,128)(2,1)}), bf16[8,16,768]{2,0,1:T(8,128)(2,1)S(1)}, u32[]{:S(2)}, u32[]{:S(2)}) async-start(bf16[8,16,768]{2,0,1:T(8,128)(2,1)} %reshape.116), calls=%async_computation.4 | async-start | bytes 393216 | tf_op jit(solution)/shard_map/all_to_all | solution.py:96
  169.6 1.0 reshape.117
  170.6 5.3 %all-to-all-done.4 = bf16[8,16,768]{2,0,1:T(8,128)(2,1)S(1)} async-done(((bf16[8,16,768]{2,0,1:T(8,128)(2,1)}), bf16[8,16,768]{2,0,1:T(8,128)(2,1)S(1)}, u32[]{:S(2)}, u32[]{:S(2)}) %all-to-all-start.4) | async-done | bytes 196640 | tf_op jit(solution)/shard_map/all_to_all | solution.py:96
  175.9 3.4 %all-to-all-start.5 = ((bf16[8,16,768]{2,0,1:T(8,128)(2,1)}), bf16[8,16,768]{2,0,1:T(8,128)(2,1)S(1)}, u32[]{:S(2)}, u32[]{:S(2)}) async-start(bf16[8,16,768]{2,0,1:T(8,128)(2,1)} %reshape.117), calls=%async_computation.5 | async-start | bytes 393216 | tf_op jit(solution)/shard_map/all_to_all | solution.py:103
  181.3 4.2 %all-to-all-done.5 = bf16[8,16,768]{2,0,1:T(8,128)(2,1)S(1)} async-done(((bf16[8,16,768]{2,0,1:T(8,128)(2,1)}), bf16[8,16,768]{2,0,1:T(8,128)(2,1)S(1)}, u32[]{:S(2)}, u32[]{:S(2)}) %all-to-all-start.5) | async-done | bytes 196640 | tf_op jit(solution)/shard_map/all_to_all | solution.py:103
  185.5 3.4 %all-to-all-start.6 = ((bf16[8,16,768]{2,0,1:T(8,128)(2,1)}), bf16[8,16,768]{2,0,1:T(8,128)(2,1)S(1)}, u32[]{:S(2)}, u32[]{:S(2)}) async-start(bf16[8,16,768]{2,0,1:T(8,128)(2,1)} %reshape.118), calls=%async_computation.6 | async-start | bytes 393216 | tf_op jit(solution)/shard_map/all_to_all | solution.py:110
  193.1 2.0 %all-to-all-done.6 = bf16[8,16,768]{2,0,1:T(8,128)(2,1)S(1)} async-done(((bf16[8,16,768]{2,0,1:T(8,128)(2,1)}), bf16[8,16,768]{2,0,1:T(8,128)(2,1)S(1)}, u32[]{:S(2)}, u32[]{:S(2)}) %all-to-all-start.6) | async-done | bytes 196640 | tf_op jit(solution)/shard_map/all_to_all | solution.py:110
  (54 shorter events, 18.8 us)
Async XLA Ops:
  2.3 4.3 %copy-start = (bf16[32,4,768]{2,1,0:T(4,128)(2,1)S(1)}, bf16[32,4,768]{2,1,0:T(4,128)(2,1)}, u32[]{:S(2)}) copy-start(bf16[32,4,768]{2,1,0:T(4,128)(2,1)} %param.15) | copy-start | bytes 589828
  2.3 9.7 %all-to-all-start.8 = ((bf16[32,4,768]{2,0,1:T(8,128)(2,1)}), bf16[32,4,768]{2,0,1:T(8,128)(2,1)S(1)}, u32[]{:S(2)}, u32[]{:S(2)}) async-start(bf16[32,4,768]{2,0,1:T(8,128)(2,1)} %copy.133), calls=%async_computation.8 | async-start | bytes 393216 | tf_op jit(solution)/shard_map/all_to_all | solution.py:123
  7.3 8.0 %copy-start.1 = (bf16[32,4,768]{2,1,0:T(4,128)(2,1)S(1)}, bf16[32,4,768]{2,1,0:T(4,128)(2,1)}, u32[]{:S(2)}) copy-start(bf16[32,4,768]{2,1,0:T(4,128)(2,1)} %param.14) | copy-start | bytes 589828
  11.9 8.7 %all-to-all-start.9 = ((bf16[32,4,768]{2,0,1:T(8,128)(2,1)}), bf16[32,4,768]{2,0,1:T(8,128)(2,1)S(1)}, u32[]{:S(2)}, u32[]{:S(2)}) async-start(bf16[32,4,768]{2,0,1:T(8,128)(2,1)} %copy.136), calls=%async_computation.9 | async-start | bytes 393216 | tf_op jit(solution)/shard_map/all_to_all | solution.py:129
  16.0 8.0 %copy-start.2 = (bf16[32,4,768]{2,1,0:T(4,128)(2,1)S(1)}, bf16[32,4,768]{2,1,0:T(4,128)(2,1)}, u32[]{:S(2)}) copy-start(bf16[32,4,768]{2,1,0:T(4,128)(2,1)} %param.12) | copy-start | bytes 589828
  20.6 8.7 %all-to-all-start.10 = ((bf16[32,4,768]{2,0,1:T(8,128)(2,1)}), bf16[32,4,768]{2,0,1:T(8,128)(2,1)S(1)}, u32[]{:S(2)}, u32[]{:S(2)}) async-start(bf16[32,4,768]{2,0,1:T(8,128)(2,1)} %copy.137), calls=%async_computation.10 | async-start | bytes 393216 | tf_op jit(solution)/shard_map/all_to_all | solution.py:126
  24.0 13.0 %copy-start.3 = (bf16[32,4,768]{2,1,0:T(4,128)(2,1)S(1)}, bf16[32,4,768]{2,1,0:T(4,128)(2,1)}, u32[]{:S(2)}) copy-start(bf16[32,4,768]{2,1,0:T(4,128)(2,1)} %param.10) | copy-start | bytes 589828
  49.7 9.7 %all-to-all-start.2 = ((bf16[32,4,768]{2,1,0:T(4,128)(2,1)}), bf16[32,4,768]{2,1,0:T(4,128)(2,1)S(1)}, u32[]{:S(2)}, u32[]{:S(2)}) async-start(bf16[32,4,768]{2,1,0:T(4,128)(2,1)} %param.11), calls=%async_computation.2 | async-start | bytes 393216 | tf_op jit(solution)/shard_map/all_to_all | solution.py:64
  59.4 9.6 %all-to-all-start.1 = ((bf16[32,4,768]{2,1,0:T(4,128)(2,1)}), bf16[32,4,768]{2,1,0:T(4,128)(2,1)S(1)}, u32[]{:S(2)}, u32[]{:S(2)}) async-start(bf16[32,4,768]{2,1,0:T(4,128)(2,1)} %param.9), calls=%async_computation.1 | async-start | bytes 393216 | tf_op jit(solution)/shard_map/all_to_all | solution.py:62
  68.9 9.8 %all-to-all-start = ((bf16[32,4,768]{2,1,0:T(4,128)(2,1)}), bf16[32,4,768]{2,1,0:T(4,128)(2,1)S(1)}, u32[]{:S(2)}, u32[]{:S(2)}) async-start(bf16[32,4,768]{2,1,0:T(4,128)(2,1)} %param.8), calls=%async_computation | async-start | bytes 393216 | tf_op jit(solution)/shard_map/all_to_all | solution.py:61
  78.7 68.9 %all-to-all-start.11 = ((bf16[4,32,768]{2,1,0:T(8,128)(2,1)}), bf16[4,32,768]{2,1,0:T(8,128)(2,1)S(1)}, u32[]{:S(2)}, u32[]{:S(2)}) async-start(bf16[4,32,768]{2,1,0:T(8,128)(2,1)} %all_to_all.191), calls=%async_computation.11 | async-start | bytes 393216 | tf_op jit(solution)/shard_map/all_to_all | solution.py:142
  147.6 8.7 %all-to-all-start.12 = ((bf16[4,32,768]{2,1,0:T(8,128)(2,1)}), bf16[4,32,768]{2,1,0:T(8,128)(2,1)S(1)}, u32[]{:S(2)}, u32[]{:S(2)}) async-start(bf16[4,32,768]{2,1,0:T(8,128)(2,1)} %all_to_all.194), calls=%async_computation.12 | async-start | bytes 393216 | tf_op jit(solution)/shard_map/all_to_all | solution.py:145
  156.3 8.7 %all-to-all-start.13 = ((bf16[4,32,768]{2,1,0:T(8,128)(2,1)}), bf16[4,32,768]{2,1,0:T(8,128)(2,1)S(1)}, u32[]{:S(2)}, u32[]{:S(2)}) async-start(bf16[4,32,768]{2,1,0:T(8,128)(2,1)} %all_to_all.197), calls=%async_computation.13 | async-start | bytes 393216 | tf_op jit(solution)/shard_map/all_to_all | solution.py:148
  165.0 10.9 %all-to-all-start.4 = ((bf16[8,16,768]{2,0,1:T(8,128)(2,1)}), bf16[8,16,768]{2,0,1:T(8,128)(2,1)S(1)}, u32[]{:S(2)}, u32[]{:S(2)}) async-start(bf16[8,16,768]{2,0,1:T(8,128)(2,1)} %reshape.116), calls=%async_computation.4 | async-start | bytes 393216 | tf_op jit(solution)/shard_map/all_to_all | solution.py:96
  175.9 9.6 %all-to-all-start.5 = ((bf16[8,16,768]{2,0,1:T(8,128)(2,1)}), bf16[8,16,768]{2,0,1:T(8,128)(2,1)S(1)}, u32[]{:S(2)}, u32[]{:S(2)}) async-start(bf16[8,16,768]{2,0,1:T(8,128)(2,1)} %reshape.117), calls=%async_computation.5 | async-start | bytes 393216 | tf_op jit(solution)/shard_map/all_to_all | solution.py:103
  185.5 9.6 %all-to-all-start.6 = ((bf16[8,16,768]{2,0,1:T(8,128)(2,1)}), bf16[8,16,768]{2,0,1:T(8,128)(2,1)S(1)}, u32[]{:S(2)}, u32[]{:S(2)}) async-start(bf16[8,16,768]{2,0,1:T(8,128)(2,1)} %reshape.118), calls=%async_computation.6 | async-start | bytes 393216 | tf_op jit(solution)/shard_map/all_to_all | solution.py:110
where the time goes:
time: 197 us; the launch traced here: 196 us
  blocking collectives  84.5 us (43%)
  starting transfers between devices  41.6 us (21%)
  waiting for transfers between devices  41.6 us (21%)
  local copies, waits for them, and re-layouts  19.9 us (10%)
  matrix products  5.4 us (3%)
    psum x1, blocking collectives, local(): scores, prob_grad = lax.psum((score_part, prob_part), ('col', 'seq'))  64.1 us
    all_to_all x1, blocking collectives, local(): lax.all_to_all(row_value, 'col', split_axis=0, concat_axis=1, tiled=True)  12.7 us
    unnamed x18, local copies, waits for them, and re-layouts  8.05 us
    all_to_all x1, blocking collectives, local(): lax.all_to_all(col_query.reshape(seq_dev, flat_width), 'seq', split_axis=...  7.69 us
    all_to_all x1, waiting for transfers between devices, local(): lax.all_to_all(row_key, 'col', split_axis=0, concat_axis=1, tiled=True)  5.42 us
    all_to_all x1, waiting for transfers between devices, local(): lax.all_to_all(query_grad.astype(jnp.bfloat16).reshape(own_rows, cols, wi...  5.29 us
    all_to_all x1, waiting for transfers between devices, local(): lax.all_to_all(col_value.reshape(seq_dev, flat_width), 'seq', split_axis=...  5.25 us
    all_to_all x1, waiting for transfers between devices, local(): lax.all_to_all(col_key.reshape(seq_dev, flat_width), 'seq', split_axis=1,...  4.63 us
  transfers between devices with their start and end apart: 12, of which 10 were waited for; matrix products, arithmetic and copies ran while one was open for 11% of the time, Pallas kernels for 0%

commit v1 on v0

--- a/solution.py
+++ b/solution.py
@@ -5,6 +5,29 @@
 
 HEADS = 12
 HEAD = 64
+
+
+def split_up(x, dim, count):
+    dims = x.shape
+    blocks = x.reshape(*dims[:dim], count, dims[dim] // count, *dims[dim + 1 :])
+    return jnp.moveaxis(blocks, dim, 0)
+
+
+def joined_along(blocks, dim):
+    blocks = jnp.moveaxis(blocks, 0, dim)
+    shape = blocks.shape
+    return blocks.reshape(*shape[:dim], shape[dim] * shape[dim + 1], *shape[dim + 2 :])
+
+
+def exchange_in_pairs(shard, axis, split_dim, concat_dim):
+    length, index = (lax.axis_size(axis), lax.axis_index(axis))
+    blocks = split_up(shard, split_dim, length)
+    gathered = [blocks[index]]
+    for hop in range(1, length):
+        sent = blocks[index ^ hop]
+        gathered.append(lax.ppermute(sent, axis, [(i, i ^ hop) for i in range(length)]))
+    blocks = jnp.stack(gathered)[index ^ jnp.arange(length)]
+    return joined_along(blocks, concat_dim)
 
 
 def tied_terms(scores, prob_grad, row_scale):
@@ -139,9 +162,7 @@
     )
     share_width = col_moved[0].shape[1]
     col_back = (
-        lax.all_to_all(
-            col_grads[0].reshape(seqs, share_width), "seq", split_axis=0, concat_axis=1, tiled=True
-        ),
+        exchange_in_pairs(col_grads[0].reshape(seqs, share_width), "seq", 0, 1),
         lax.all_to_all(
             col_grads[1].reshape(seqs, share_width), "seq", split_axis=0, concat_axis=1, tiled=True
         ),

time: 197 us -> 196 us (level)
  waiting for transfers between devices: 41.6 us -> 35.2 us
  matrix products: 5.4 us -> 9.11 us
  local copies, waits for them, and re-layouts: 19.9 us -> 21.9 us
    all_to_all x1 -> x0, starting transfers between devices: 3.38 us -> none  [local(): lax.all_to_all(col_grads[0].reshape(seqs, share_width), 'seq', split_axis...]
    all_to_all x1, waiting for transfers between devices: 3.37 us -> 0.01 us  [local(): lax.all_to_all(col_grads[1].reshape(seqs, share_width), 'seq', split_axis...]
    all_to_all x1, waiting for transfers between devices: 4.22 us -> 0.93 us  [local(): lax.all_to_all(key_gradient_part.astype(jnp.bfloat16).reshape(own_rows, c...]
    ppermute x0 -> x3, waiting for transfers between devices: none -> 2.7 us  [exchange_in_pairs(): lax.ppermute(sent, axis, [(i, i ^ hop) for i in range(length)])]
    all_to_all x1, waiting for transfers between devices: 2.02 us -> 0.01 us  [local(): lax.all_to_all(value_gradient_part.astype(jnp.bfloat16).reshape(own_rows,...]
    unnamed x18 -> x36, local copies, waits for them, and re-layouts: 8.05 us -> 9.34 us
  transfers between devices with their start and end apart: 12 -> 14, of which waited for: 10 -> 10; matrix products, arithmetic and copies ran while one was open for 11% -> 14% of each run, Pallas kernels for 0% -> 0%
where the time goes in v1:
time: 196 us; the launch traced here: 195 us
  blocking collectives  84.6 us (43%)
  starting transfers between devices  40.8 us (21%)
  waiting for transfers between devices  35.2 us (18%)
  local copies, waits for them, and re-layouts  21.9 us (11%)
  matrix products  9.11 us (5%)
  other arithmetic  1.97 us (1%)
    psum x1, blocking collectives, local(): scores, prob_grad = lax.psum((score_part, prob_part), ('col', 'seq'))  64.2 us
    all_to_all x1, blocking collectives, local(): lax.all_to_all(row_value, 'col', split_axis=0, concat_axis=1, tiled=True)  12.7 us
    unnamed x36, local copies, waits for them, and re-layouts  9.34 us
    all_to_all x1, blocking collectives, local(): lax.all_to_all(col_query.reshape(seq_dev, flat_width), 'seq', split_axis=...  7.69 us
    all_to_all x1, waiting for transfers between devices, local(): lax.all_to_all(query_grad.astype(jnp.bfloat16).reshape(own_rows, cols, wi...  5.42 us
    all_to_all x1, waiting for transfers between devices, local(): lax.all_to_all(col_value.reshape(seq_dev, flat_width), 'seq', split_axis=...  5.25 us
    all_to_all x1, waiting for transfers between devices, local(): lax.all_to_all(row_grad, 'col', split_axis=0, concat_axis=1, tiled=True)  4.84 us
    all_to_all x1, waiting for transfers between devices, local(): lax.all_to_all(col_key.reshape(seq_dev, flat_width), 'seq', split_axis=1,...  4.63 us
  transfers between devices with their start and end apart: 14, of which 10 were waited for; matrix products, arithmetic and copies ran while one was open for 14% of the time, Pallas kernels for 0%

profile of v1, /device:TPU:0, one launch (start us, length us, event | category | flops | bytes accessed | tf_op | source)
XLA Modules:
  0.0 194.7 jit_solution(4754480474658435658)
XLA Ops:
  0.6 1.6 copy.132
  2.3 4.3 %all-to-all-start.8 = ((bf16[32,4,768]{2,0,1:T(8,128)(2,1)}), bf16[32,4,768]{2,0,1:T(8,128)(2,1)S(1)}, u32[]{:S(2)}, u32[]{:S(2)}) async-start(bf16[32,4,768]{2,0,1:T(8,128)(2,1)} %copy.132), calls=%async_computation.8 | async-start | bytes 393216 | tf_op jit(solution)/shard_map/all_to_all | solution.py:146
  7.3 4.6 %all-to-all-done.8 = bf16[32,4,768]{2,0,1:T(8,128)(2,1)S(1)} async-done(((bf16[32,4,768]{2,0,1:T(8,128)(2,1)}), bf16[32,4,768]{2,0,1:T(8,128)(2,1)S(1)}, u32[]{:S(2)}, u32[]{:S(2)}) %all-to-all-start.8) | async-done | bytes 196640 | tf_op jit(solution)/shard_map/all_to_all | solution.py:146
  11.9 3.4 %all-to-all-start.9 = ((bf16[32,4,768]{2,0,1:T(8,128)(2,1)}), bf16[32,4,768]{2,0,1:T(8,128)(2,1)S(1)}, u32[]{:S(2)}, u32[]{:S(2)}) async-start(bf16[32,4,768]{2,0,1:T(8,128)(2,1)} %copy.135), calls=%async_computation.9 | async-start | bytes 393216 | tf_op jit(solution)/shard_map/all_to_all | solution.py:152
  16.0 4.6 %all-to-all-done.9 = bf16[32,4,768]{2,0,1:T(8,128)(2,1)S(1)} async-done(((bf16[32,4,768]{2,0,1:T(8,128)(2,1)}), bf16[32,4,768]{2,0,1:T(8,128)(2,1)S(1)}, u32[]{:S(2)}, u32[]{:S(2)}) %all-to-all-start.9) | async-done | bytes 196640 | tf_op jit(solution)/shard_map/all_to_all | solution.py:152
  20.6 3.4 %all-to-all-start.10 = ((bf16[32,4,768]{2,0,1:T(8,128)(2,1)}), bf16[32,4,768]{2,0,1:T(8,128)(2,1)S(1)}, u32[]{:S(2)}, u32[]{:S(2)}) async-start(bf16[32,4,768]{2,0,1:T(8,128)(2,1)} %copy.136), calls=%async_computation.10 | async-start | bytes 393216 | tf_op jit(solution)/shard_map/all_to_all | solution.py:149
  24.0 5.2 %all-to-all-done.10 = bf16[32,4,768]{2,0,1:T(8,128)(2,1)S(1)} async-done(((bf16[32,4,768]{2,0,1:T(8,128)(2,1)}), bf16[32,4,768]{2,0,1:T(8,128)(2,1)S(1)}, u32[]{:S(2)}, u32[]{:S(2)}) %all-to-all-start.10) | async-done | bytes 196640 | tf_op jit(solution)/shard_map/all_to_all | solution.py:149
  29.3 7.7 %all_to_all.198 = bf16[32,4,768]{2,0,1:T(8,128)(2,1)S(1)} all-to-all(bf16[32,4,768]{2,0,1:T(8,128)(2,1)S(1)} %copy.131), channel_id=1, replica_groups=mesh['grp'=2,'col'=4,'seq'=4] {'seq'}, dimensions={1} | all-to-all | bytes 393216 | tf_op jit(solution)/shard_map/all_to_all | solution.py:143
  37.0 12.7 %all_to_all.199 = bf16[32,4,768]{2,1,0:T(4,128)(2,1)S(1)} all-to-all(bf16[32,4,768]{2,1,0:T(4,128)(2,1)S(1)} %copy-done.8), channel_id=1, replica_groups=mesh['grp'=2,'col'=4,'seq'=4] {'col'}, dimensions={0} | all-to-all | bytes 393216 | tf_op jit(solution)/shard_map/all_to_all | solution.py:86
  49.7 3.4 %all-to-all-start.2 = ((bf16[32,4,768]{2,1,0:T(4,128)(2,1)}), bf16[32,4,768]{2,1,0:T(4,128)(2,1)S(1)}, u32[]{:S(2)}, u32[]{:S(2)}) async-start(bf16[32,4,768]{2,1,0:T(4,128)(2,1)} %param.11), calls=%async_computation.2 | async-start | bytes 393216 | tf_op jit(solution)/shard_map/all_to_all | solution.py:87
  54.5 4.8 %all-to-all-done.2 = bf16[32,4,768]{2,1,0:T(4,128)(2,1)S(1)} async-done(((bf16[32,4,768]{2,1,0:T(4,128)(2,1)}), bf16[32,4,768]{2,1,0:T(4,128)(2,1)S(1)}, u32[]{:S(2)}, u32[]{:S(2)}) %all-to-all-start.2) | async-done | bytes 196640 | tf_op jit(solution)/shard_map/all_to_all | solution.py:87
  59.4 3.4 %all-to-all-start.1 = ((bf16[32,4,768]{2,1,0:T(4,128)(2,1)}), bf16[32,4,768]{2,1,0:T(4,128)(2,1)S(1)}, u32[]{:S(2)}, u32[]{:S(2)}) async-start(bf16[32,4,768]{2,1,0:T(4,128)(2,1)} %param.9), calls=%async_computation.1 | async-start | bytes 393216 | tf_op jit(solution)/shard_map/all_to_all | solution.py:85
  62.7 1.3 fusion.60
  65.4 3.6 %all-to-all-done.1 = bf16[32,4,768]{2,1,0:T(4,128)(2,1)S(1)} async-done(((bf16[32,4,768]{2,1,0:T(4,128)(2,1)}), bf16[32,4,768]{2,1,0:T(4,128)(2,1)S(1)}, u32[]{:S(2)}, u32[]{:S(2)}) %all-to-all-start.1) | async-done | bytes 196640 | tf_op jit(solution)/shard_map/all_to_all | solution.py:85
  68.9 3.4 %all-to-all-start = ((bf16[32,4,768]{2,1,0:T(4,128)(2,1)}), bf16[32,4,768]{2,1,0:T(4,128)(2,1)S(1)}, u32[]{:S(2)}, u32[]{:S(2)}) async-start(bf16[32,4,768]{2,1,0:T(4,128)(2,1)} %param.8), calls=%async_computation | async-start | bytes 393216 | tf_op jit(solution)/shard_map/all_to_all | solution.py:84
  72.3 1.8 fusion.13
  77.6 1.1 reshape.112
  79.5 3.4 %all-to-all-start.11 = ((bf16[4,32,768]{2,1,0:T(8,128)(2,1)}), bf16[4,32,768]{2,1,0:T(8,128)(2,1)S(1)}, u32[]{:S(2)}, u32[]{:S(2)}) async-start(bf16[4,32,768]{2,1,0:T(8,128)(2,1)} %all_to_all.179), calls=%async_computation.11 | async-start | bytes 393216 | tf_op jit(solution)/shard_map/all_to_all | solution.py:166
  85.0 64.2 %all-reduce = (f32[12,16,16]{2,1,0:T(8,128)S(1)}, f32[12,16,16]{2,1,0:T(8,128)S(1)}) all-reduce(f32[12,16,16]{2,1,0:T(8,128)S(1)} %convolution_bitcast_fusion, f32[12,16,16]{2,1,0:T(8,128)S(1)} %fusion.21), channel_id=1, replica_groups=mesh['grp'=2,'col'=4,'seq'=4] {'col','seq'}, use_global_device_ids=true, to_apply=%region_3.0 | all-reduce | flops 6144 | bytes 49152 | tf_op jit(solution)/shard_map/psum | solution.py:104
  149.3 1.9 fusion.59
  151.2 3.4 %all-to-all-start.12 = ((bf16[4,32,768]{2,1,0:T(8,128)(2,1)}), bf16[4,32,768]{2,1,0:T(8,128)(2,1)S(1)}, u32[]{:S(2)}, u32[]{:S(2)}) async-start(bf16[4,32,768]{2,1,0:T(8,128)(2,1)} %all_to_all.182), calls=%async_computation.12 | async-start | bytes 393216 | tf_op jit(solution)/shard_map/all_to_all | solution.py:169
  155.7 1.0 reshape.133
  156.7 3.3 %all-to-all-done.12 = bf16[4,32,768]{2,1,0:T(8,128)(2,1)S(1)} async-done(((bf16[4,32,768]{2,1,0:T(8,128)(2,1)}), bf16[4,32,768]{2,1,0:T(8,128)(2,1)S(1)}, u32[]{:S(2)}, u32[]{:S(2)}) %all-to-all-start.12) | async-done | bytes 196640 | tf_op jit(solution)/shard_map/all_to_all | solution.py:169
  159.9 3.4 %all-to-all-start.4 = ((bf16[8,16,768]{2,0,1:T(8,128)(2,1)}), bf16[8,16,768]{2,0,1:T(8,128)(2,1)S(1)}, u32[]{:S(2)}, u32[]{:S(2)}) async-start(bf16[8,16,768]{2,0,1:T(8,128)(2,1)} %reshape.133), calls=%async_computation.4 | async-start | bytes 393216 | tf_op jit(solution)/shard_map/all_to_all | solution.py:119
  164.5 1.0 reshape.134
  165.5 5.4 %all-to-all-done.4 = bf16[8,16,768]{2,0,1:T(8,128)(2,1)S(1)} async-done(((bf16[8,16,768]{2,0,1:T(8,128)(2,1)}), bf16[8,16,768]{2,0,1:T(8,128)(2,1)S(1)}, u32[]{:S(2)}, u32[]{:S(2)}) %all-to-all-start.4) | async-done | bytes 196640 | tf_op jit(solution)/shard_map/all_to_all | solution.py:119
  170.9 3.5 %all-to-all-start.5 = ((bf16[8,16,768]{2,0,1:T(8,128)(2,1)}), bf16[8,16,768]{2,0,1:T(8,128)(2,1)S(1)}, u32[]{:S(2)}, u32[]{:S(2)}) async-start(bf16[8,16,768]{2,0,1:T(8,128)(2,1)} %reshape.134), calls=%async_computation.5 | async-start | bytes 393216 | tf_op jit(solution)/shard_map/all_to_all | solution.py:126
  174.5 1.7 fusion.15
  180.5 3.9 %all-to-all-start.6 = ((bf16[8,16,768]{2,0,1:T(8,128)(2,1)}), bf16[8,16,768]{2,0,1:T(8,128)(2,1)S(1)}, u32[]{:S(2)}, u32[]{:S(2)}) async-start(bf16[8,16,768]{2,0,1:T(8,128)(2,1)} %reshape.135), calls=%async_computation.6 | async-start | bytes 393216 | tf_op jit(solution)/shard_map/all_to_all | solution.py:133
  185.2 1.2 collective-permute-start
  186.4 1.6 collective-permute-done.2
  188.0 1.1 collective-permute-done.1
  (81 shorter events, 23.2 us)
Async XLA Ops:
  2.3 4.3 %copy-start.5 = (bf16[32,4,768]{2,1,0:T(4,128)(2,1)S(1)}, bf16[32,4,768]{2,1,0:T(4,128)(2,1)}, u32[]{:S(2)}) copy-start(bf16[32,4,768]{2,1,0:T(4,128)(2,1)} %param.15) | copy-start | bytes 589828
  2.3 9.7 %all-to-all-start.8 = ((bf16[32,4,768]{2,0,1:T(8,128)(2,1)}), bf16[32,4,768]{2,0,1:T(8,128)(2,1)S(1)}, u32[]{:S(2)}, u32[]{:S(2)}) async-start(bf16[32,4,768]{2,0,1:T(8,128)(2,1)} %copy.132), calls=%async_computation.8 | async-start | bytes 393216 | tf_op jit(solution)/shard_map/all_to_all | solution.py:146
  7.3 8.0 %copy-start.6 = (bf16[32,4,768]{2,1,0:T(4,128)(2,1)S(1)}, bf16[32,4,768]{2,1,0:T(4,128)(2,1)}, u32[]{:S(2)}) copy-start(bf16[32,4,768]{2,1,0:T(4,128)(2,1)} %param.14) | copy-start | bytes 589828
  11.9 8.7 %all-to-all-start.9 = ((bf16[32,4,768]{2,0,1:T(8,128)(2,1)}), bf16[32,4,768]{2,0,1:T(8,128)(2,1)S(1)}, u32[]{:S(2)}, u32[]{:S(2)}) async-start(bf16[32,4,768]{2,0,1:T(8,128)(2,1)} %copy.135), calls=%async_computation.9 | async-start | bytes 393216 | tf_op jit(solution)/shard_map/all_to_all | solution.py:152
  16.0 8.0 %copy-start.7 = (bf16[32,4,768]{2,1,0:T(4,128)(2,1)S(1)}, bf16[32,4,768]{2,1,0:T(4,128)(2,1)}, u32[]{:S(2)}) copy-start(bf16[32,4,768]{2,1,0:T(4,128)(2,1)} %param.12) | copy-start | bytes 589828
  20.6 8.7 %all-to-all-start.10 = ((bf16[32,4,768]{2,0,1:T(8,128)(2,1)}), bf16[32,4,768]{2,0,1:T(8,128)(2,1)S(1)}, u32[]{:S(2)}, u32[]{:S(2)}) async-start(bf16[32,4,768]{2,0,1:T(8,128)(2,1)} %copy.136), calls=%async_computation.10 | async-start | bytes 393216 | tf_op jit(solution)/shard_map/all_to_all | solution.py:149
  24.0 13.0 %copy-start.8 = (bf16[32,4,768]{2,1,0:T(4,128)(2,1)S(1)}, bf16[32,4,768]{2,1,0:T(4,128)(2,1)}, u32[]{:S(2)}) copy-start(bf16[32,4,768]{2,1,0:T(4,128)(2,1)} %param.10) | copy-start | bytes 589828
  49.7 9.7 %all-to-all-start.2 = ((bf16[32,4,768]{2,1,0:T(4,128)(2,1)}), bf16[32,4,768]{2,1,0:T(4,128)(2,1)S(1)}, u32[]{:S(2)}, u32[]{:S(2)}) async-start(bf16[32,4,768]{2,1,0:T(4,128)(2,1)} %param.11), calls=%async_computation.2 | async-start | bytes 393216 | tf_op jit(solution)/shard_map/all_to_all | solution.py:87
  53.8 21.7 %copy-start.9 = (bf16[128,12,64]{0,2,1:T(8,128)(2,1)}, bf16[128,12,64]{0,2,1:T(8,128)(2,1)S(1)}, u32[]{:S(2)}) copy-start(bf16[128,12,64]{0,2,1:T(8,128)(2,1)S(1)} %copy.134) | copy-start | bytes 589828
  59.4 9.6 %all-to-all-start.1 = ((bf16[32,4,768]{2,1,0:T(4,128)(2,1)}), bf16[32,4,768]{2,1,0:T(4,128)(2,1)S(1)}, u32[]{:S(2)}, u32[]{:S(2)}) async-start(bf16[32,4,768]{2,1,0:T(4,128)(2,1)} %param.9), calls=%async_computation.1 | async-start | bytes 393216 | tf_op jit(solution)/shard_map/all_to_all | solution.py:85
  64.0 11.5 %copy-start.11 = (f32[12,128]{1,0:T(8,128)}, f32[12,128]{1,0:T(8,128)S(1)}, u32[]{:S(2)}) copy-start(f32[12,128]{1,0:T(8,128)S(1)} %get-tuple-element.32) | copy-start | bytes 18436
  68.9 10.5 %all-to-all-start = ((bf16[32,4,768]{2,1,0:T(4,128)(2,1)}), bf16[32,4,768]{2,1,0:T(4,128)(2,1)S(1)}, u32[]{:S(2)}, u32[]{:S(2)}) async-start(bf16[32,4,768]{2,1,0:T(4,128)(2,1)} %param.8), calls=%async_computation | async-start | bytes 393216 | tf_op jit(solution)/shard_map/all_to_all | solution.py:84
  79.5 5.0 %copy-start = (bf16[8,16,12,64]{3,2,0,1:T(8,128)(2,1)}, bf16[8,16,12,64]{3,2,0,1:T(8,128)(2,1)S(1)}, u32[]{:S(2)}) copy-start(bf16[8,16,12,64]{3,2,0,1:T(8,128)(2,1)S(1)} %reshape.110) | copy-start | bytes 589828
  79.5 71.7 %all-to-all-start.11 = ((bf16[4,32,768]{2,1,0:T(8,128)(2,1)}), bf16[4,32,768]{2,1,0:T(8,128)(2,1)S(1)}, u32[]{:S(2)}, u32[]{:S(2)}) async-start(bf16[4,32,768]{2,1,0:T(8,128)(2,1)} %all_to_all.179), calls=%async_computation.11 | async-start | bytes 393216 | tf_op jit(solution)/shard_map/all_to_all | solution.py:166
  82.9 1.0 copy-start.2
  85.0 69.6 %copy-start.1 = (bf16[8,16,12,64]{3,2,0,1:T(8,128)(2,1)S(1)}, bf16[8,16,12,64]{3,2,0,1:T(8,128)(2,1)}, u32[]{:S(2)}) copy-start(bf16[8,16,12,64]{3,2,0,1:T(8,128)(2,1)} %copy-done) | copy-start | bytes 589828
  149.2 1.9 copy-start.3
  151.2 8.7 %all-to-all-start.12 = ((bf16[4,32,768]{2,1,0:T(8,128)(2,1)}), bf16[4,32,768]{2,1,0:T(8,128)(2,1)S(1)}, u32[]{:S(2)}, u32[]{:S(2)}) async-start(bf16[4,32,768]{2,1,0:T(8,128)(2,1)} %all_to_all.182), calls=%async_computation.12 | async-start | bytes 393216 | tf_op jit(solution)/shard_map/all_to_all | solution.py:169
  159.9 10.9 %all-to-all-start.4 = ((bf16[8,16,768]{2,0,1:T(8,128)(2,1)}), bf16[8,16,768]{2,0,1:T(8,128)(2,1)S(1)}, u32[]{:S(2)}, u32[]{:S(2)}) async-start(bf16[8,16,768]{2,0,1:T(8,128)(2,1)} %reshape.133), calls=%async_computation.4 | async-start | bytes 393216 | tf_op jit(solution)/shard_map/all_to_all | solution.py:119
  165.5 9.0 %copy-start.10 = (bf16[128,12,64]{0,2,1:T(8,128)(2,1)S(1)}, bf16[128,12,64]{0,2,1:T(8,128)(2,1)}, u32[]{:S(2)}) copy-start(bf16[128,12,64]{0,2,1:T(8,128)(2,1)} %copy-done.9) | copy-start | bytes 589828
  165.5 9.0 %copy-start.12 = (f32[12,128]{1,0:T(8,128)S(1)}, f32[12,128]{1,0:T(8,128)}, u32[]{:S(2)}) copy-start(f32[12,128]{1,0:T(8,128)} %copy-done.11) | copy-start | bytes 18436
  170.9 9.6 %all-to-all-start.5 = ((bf16[8,16,768]{2,0,1:T(8,128)(2,1)}), bf16[8,16,768]{2,0,1:T(8,128)(2,1)S(1)}, u32[]{:S(2)}, u32[]{:S(2)}) async-start(bf16[8,16,768]{2,0,1:T(8,128)(2,1)} %reshape.134), calls=%async_computation.5 | async-start | bytes 393216 | tf_op jit(solution)/shard_map/all_to_all | solution.py:126
  176.7 0.9 copy-start.4
  180.5 13.4 %all-to-all-start.6 = ((bf16[8,16,768]{2,0,1:T(8,128)(2,1)}), bf16[8,16,768]{2,0,1:T(8,128)(2,1)S(1)}, u32[]{:S(2)}, u32[]{:S(2)}) async-start(bf16[8,16,768]{2,0,1:T(8,128)(2,1)} %reshape.135), calls=%async_computation.6 | async-start | bytes 393216 | tf_op jit(solution)/shard_map/all_to_all | solution.py:133
  184.4 3.6 %collective-permute-start.2 = (bf16[32,768]{1,0:T(8,128)(2,1)S(1)}, bf16[32,768]{1,0:T(8,128)(2,1)S(1)}, u32[]{:S(2)}, u32[]{:S(2)}) collective-permute-start(bf16[32,768]{1,0:T(8,128)(2,1)S(1)} %get-tuple-element.27), channel_id=1, source_target_pairs={{0,3},{1,2},{2,1},{3,0},{4,7},{5,6},{6,5},{7,4},{8,11},{9,10},{10,... | collective-permute-start | bytes 147464 | tf_op jit(solution)/shard_map/ppermute | solution.py:28
  184.5 4.6 %collective-permute-start.1 = (bf16[32,768]{1,0:T(8,128)(2,1)S(1)}, bf16[32,768]{1,0:T(8,128)(2,1)S(1)}, u32[]{:S(2)}, u32[]{:S(2)}) collective-permute-start(bf16[32,768]{1,0:T(8,128)(2,1)S(1)} %get-tuple-element.28), channel_id=1, source_target_pairs={{0,2},{1,3},{2,0},{3,1},{4,6},{5,7},{6,4},{7,5},{8,10},{9,11},{10,... | collective-permute-start | bytes 147464 | tf_op jit(solution)/shard_map/ppermute | solution.py:28
  185.2 3.9 %collective-permute-start = (bf16[32,768]{1,0:T(8,128)(2,1)S(1)}, bf16[32,768]{1,0:T(8,128)(2,1)S(1)}, u32[]{:S(2)}, u32[]{:S(2)}) collective-permute-start(bf16[32,768]{1,0:T(8,128)(2,1)S(1)} %get-tuple-element.29), channel_id=1, source_target_pairs={{0,1},{1,0},{2,3},{3,2},{4,5},{5,4},{6,7},{7,6},{8,9},{9,8},{10,11... | collective-permute-start | bytes 147464 | tf_op jit(solution)/shard_map/ppermute | solution.py:28
